TPU v7x, 32 devices: a whole 2x2x4 slice. The times are simulated.
32 devices in a mesh: row: 8 (over y, x, core), col: 4 (over z).
Axes of the slice: x: 2, y: 2, z: 4, core: 2. Of those that a mesh axis runs over, the one named last changes fastest.
Arguments:
- front_matrix: bfloat16 [20480, 20480], P('row', 'col'), may hold values from -37 to 37
- right_samples: bfloat16 [20480, 256], P('col'), may hold values from -0.0390625 to 0.0390625
- left_samples: bfloat16 [20480, 256], P('row'), may hold values from -0.0390625 to 0.0390625
Outputs:
- residual: bfloat16 [20480, 20480], P('row', 'col')
- core_scaled: float32 [256, 256], replicated
All inputs are finite; a program needn't handle non-finite values.
Results may differ from a plain program's by a relative error of at most 0.0035.
Values may be sent and summed in bfloat16 or wider, within the bound.
A program may use at most 128 MiB of HBM per device.

v0:
```python
import jax
import jax.numpy as jnp
from jax import lax
from jax.sharding import PartitionSpec as P

ORDER = 20480


def gram_matrix(sketch):
    return lax.dot_general(
        sketch,
        sketch,
        (((0,), (0,)), ((), ())),
        precision=lax.Precision.HIGHEST,
        preferred_element_type=jnp.float32,
    )


def orthonormal(sketch, gram_total):
    lower_factor = jnp.linalg.cholesky(gram_total)
    return jax.scipy.linalg.solve_triangular(lower_factor, sketch.T, lower=True).T


def core_part(basis_rows, applied):
    return lax.dot_general(
        basis_rows.astype(jnp.float32),
        applied,
        (((0,), (0,)), ((), ())),
        precision=lax.Precision.HIGHEST,
        preferred_element_type=jnp.float32,
    )


def body(front_matrix, right_samples, left_samples):
    sketch_rows = jnp.dot(front_matrix, right_samples, preferred_element_type=jnp.float32)
    sketch_rows = lax.psum(sketch_rows, "col")
    sketch_cols = lax.dot_general(
        front_matrix, left_samples, (((0,), (0,)), ((), ())), preferred_element_type=jnp.float32
    )
    sketch_cols = lax.psum(sketch_cols, "row")
    gram_rows = lax.psum(gram_matrix(sketch_rows), "row")
    gram_cols = lax.psum(gram_matrix(sketch_cols), "col")
    basis_rows = orthonormal(sketch_rows, gram_rows).astype(jnp.bfloat16)
    basis_cols = orthonormal(sketch_cols, gram_cols).astype(jnp.bfloat16)
    applied = jnp.dot(front_matrix, basis_cols, preferred_element_type=jnp.float32)
    applied = lax.psum(applied, "col")
    core_matrix = lax.psum(core_part(basis_rows, applied), "row")
    core_scaled = core_matrix / jnp.sqrt(jnp.float32(ORDER))
    projected = jnp.dot(
        basis_rows.astype(jnp.float32),
        core_matrix,
        precision=lax.Precision.HIGHEST,
        preferred_element_type=jnp.float32,
    ).astype(jnp.bfloat16)
    update = lax.dot_general(
        projected, basis_cols, (((1,), (1,)), ((), ())), preferred_element_type=jnp.float32
    )
    residual = (front_matrix.astype(jnp.float32) - update).astype(jnp.bfloat16)
    return (residual, core_scaled)


def solution(mesh):
    in_specs = (P("row", "col"), P("col", None), P("row", None))
    out_specs = (P("row", "col"), P())
    return jax.shard_map(body, mesh=mesh, in_specs=in_specs, out_specs=out_specs, check_vma=False)
```

profile of v0, /device:TPU:0, one launch (start us, length us, event | category | flops | bytes accessed | tf_op | source)
XLA Modules:
  0.0 564.6 jit_solution(6918856674153980759)
XLA Ops:
  7.2 0.0 copy-start
  7.2 0.0 all-reduce.8.cloned.1.call-start
  7.2 1.7 copy-done
  8.9 13.5 %fusion.23 = f32[2560,256]{1,0:T(8,128)} fusion(bf16[2560,5120]{1,0:T(8,128)(2,1)} %param.4, bf16[5120,256]{1,0:T(8,128)(2,1)S(1)} %copy-done), kind=kOutput, calls=%fused_computation.65 | convolution fusion | flops 6710886400 | bytes 31457280 | tf_op jit(solution)/shard_map/dot_general | solution.py:35
  22.4 0.0 all-reduce.8.cloned.1.call-update
  22.5 0.0 all-reduce.16.cloned.1.call-start
  22.5 1.2 copy-done.10
  23.8 15.1 %fusion.25 = f32[5120,256]{1,0:T(8,128)} fusion(bf16[2560,5120]{1,0:T(8,128)(2,1)} %param.4, bf16[2560,256]{1,0:T(8,128)(2,1)S(1)} %copy-done.10), kind=kOutput, calls=%fused_computation.67 | convolution fusion | flops 6710886400 | bytes 32768000 | tf_op jit(solution)/shard_map/dot_general | solution.py:37
  38.8 90.6 %all-reduce.8.cloned.1.call-done = f32[2560,256]{1,0:T(8,128)} async-done(((f32[2560,256]{1,0:T(8,128)}), f32[2560,256]{1,0:T(8,128)}) %all-reduce.8.cloned.1.call-update) | async-done | bytes 2621456 | tf_op jit(solution)/shard_map/psum | solution.py:36
  129.4 7.5 %fusion.24 = f32[256,256]{0,1:T(8,128)} fusion(f32[2560,256]{1,0:T(8,128)} %all-reduce.8.cloned.1.call-done), kind=kOutput, calls=%fused_computation.66 | convolution fusion | flops 2013265920 | bytes 2883584 | tf_op jit(solution)/shard_map/dot_general | solution.py:10
  136.9 0.0 all-reduce.16.cloned.1.call-update
  136.9 0.3 all-reduce.10.cloned.1.call-start
  137.2 94.2 %all-reduce.16.cloned.1.call-done = (f32[5120,256]{1,0:T(8,128)}, f32[256,256]{0,1:T(8,128)}) async-done(((f32[5120,256]{1,0:T(8,128)}, f32[256,256]{0,1:T(8,128)}), (f32[5120,256]{1,0:T(8,128)}, f32[256,256]{0,1:T(8,128)})) %all-reduce.16.cloned.1.call-update) | async-done | bytes 5505040 | tf_op jit(solution)/shard_map/psum | solution.py:40
  231.4 13.1 %fusion.26 = f32[256,256]{0,1:T(8,128)} fusion(f32[5120,256]{1,0:T(8,128)} %get-tuple-element.35), kind=kOutput, calls=%fused_computation.68 | convolution fusion | flops 4026531840 | bytes 5505024 | tf_op jit(solution)/shard_map/dot_general | solution.py:10
  244.6 0.0 all-reduce.10.cloned.1.call-update
  244.6 0.5 all-reduce.12.cloned.1.call-start
  245.1 0.1 copy.6
  245.3 11.7 %cholesky.130 = f32[128,128]{1,0:T(8,128)S(1)} custom-call(f32[128,128]{1,0:T(8,128)S(1)} %cholesky.194), custom_call_target="Cholesky" | custom-call | tf_op jit(solution)/shard_map/jit(cholesky)/cholesky | solution.py:20
  257.0 10.4 %custom-call.19 = f32[1,128,128]{1,2,0:T(8,128)} custom-call(f32[1,128,128]{2,1,0:T(8,128)S(1)} %get-tuple-element.44), custom_call_target="InvertDiagBlocksLowerTriangular" | custom-call | tf_op jit(solution)/shard_map/jit(cholesky)/cholesky | solution.py:20
  267.5 12.9 %all-reduce.10.cloned.1.call-done = f32[256,256]{0,1:T(8,128)} async-done(((f32[256,256]{0,1:T(8,128)}), f32[256,256]{0,1:T(8,128)}) %all-reduce.10.cloned.1.call-update) | async-done | bytes 262160 | tf_op jit(solution)/shard_map/psum | solution.py:42
  280.4 1.1 copy.8
  281.5 1.0 fusion.5
  282.5 11.7 %cholesky.164 = f32[128,128]{1,0:T(8,128)S(1)} custom-call(f32[128,128]{1,0:T(8,128)S(1)} %cholesky.197), custom_call_target="Cholesky" | custom-call | tf_op jit(solution)/shard_map/jit(cholesky)/cholesky | solution.py:20
  294.2 10.0 %custom-call.20 = f32[1,128,128]{1,2,0:T(8,128)S(1)} custom-call(f32[1,128,128]{2,1,0:T(8,128)S(1)} %get-tuple-element.48), custom_call_target="InvertDiagBlocksLowerTriangular" | custom-call | tf_op jit(solution)/shard_map/jit(cholesky)/cholesky | solution.py:20
  304.2 0.2 constant_dynamic-update-slice_fusion.1
  304.4 0.3 convolution_subtract_fusion.2
  304.7 11.7 %cholesky.181 = f32[128,128]{1,0:T(8,128)S(1)} custom-call(f32[128,128]{1,0:T(8,128)S(1)} %convolution_subtract_fusion.2), custom_call_target="Cholesky" | custom-call | tf_op jit(solution)/shard_map/jit(cholesky)/cholesky | solution.py:20
  316.5 0.6 compare_reduce_fusion
  318.4 0.1 triangular_solve.96
  318.5 4.0 while.3
  318.6 0.6 fusion.50
  319.1 1.4 bitcast_dynamic-update-slice_fusion.5
  320.6 0.6 fusion.50
  321.1 1.4 bitcast_dynamic-update-slice_fusion.5
  322.5 19.7 %custom-call.17 = f32[2,128,128]{1,2,0:T(8,128)S(1)} custom-call(f32[2,128,128]{2,1,0:T(8,128)S(1)} %get-tuple-element.18), custom_call_target="InvertDiagBlocksLowerTriangular" | custom-call | tf_op jit(solution)/shard_map/jit(_solve_triangular)/triangular_solve | solution.py:21
  342.2 5.4 fusion.21
  347.6 4.4 convolution_subtract_fusion
  352.1 0.0 copy-start.4
  352.1 2.4 convolution_convert_fusion
  354.5 1.1 copy-done.5
  355.6 13.7 %convolution_bitcast_fusion = f32[2560,256]{0,1:T(8,128)} fusion(bf16[2560,5120]{1,0:T(8,128)(2,1)} %param.4, bf16[128,5120]{1,0:T(8,128)(2,1)S(1)} %convolution_convert_fusion, bf16[128,5120]{1,0:T(8,128)(2,1)S(1)} %copy-done.4), kind=kOutput, calls=%fused_computation.7 | convolution fusion | flops 6716129280 | bytes 31457280 | tf_op jit(solution)/shard_map/dot_general | solution.py:45
  369.3 0.0 all-reduce.12.cloned.1.call-update
  369.3 0.0 all-reduce.14.cloned.1.call-start
  369.4 0.2 constant_dynamic-update-slice_fusion.3
  369.6 0.3 convolution_subtract_fusion.3
  369.8 11.7 %cholesky.147 = f32[128,128]{1,0:T(8,128)S(1)} custom-call(f32[128,128]{1,0:T(8,128)S(1)} %convolution_subtract_fusion.3), custom_call_target="Cholesky" | custom-call | tf_op jit(solution)/shard_map/jit(cholesky)/cholesky | solution.py:20
  381.6 0.6 compare_reduce_fusion.2
  383.5 4.1 while.2
  383.8 0.6 fusion.49
  384.4 1.3 bitcast_dynamic-update-slice_fusion.4
  385.7 0.6 fusion.49
  386.3 1.3 bitcast_dynamic-update-slice_fusion.4
  387.6 20.3 %custom-call.16 = f32[2,128,128]{1,2,0:T(8,128)} custom-call(f32[2,128,128]{2,1,0:T(8,128)S(1)} %get-tuple-element.10), custom_call_target="InvertDiagBlocksLowerTriangular" | custom-call | tf_op jit(solution)/shard_map/jit(_solve_triangular)/triangular_solve | solution.py:21
  407.9 2.1 fusion.22
  410.0 0.0 copy-start.8
  410.1 2.2 convolution_subtract_fusion.1
  412.3 1.3 convolution_convert_fusion.2
  413.6 59.9 %all-reduce.12.cloned.1.call-done = f32[2560,256]{0,1:T(8,128)} async-done(((f32[2560,256]{0,1:T(8,128)}), f32[2560,256]{0,1:T(8,128)}) %all-reduce.12.cloned.1.call-update) | async-done | bytes 2621456 | tf_op jit(solution)/shard_map/psum | solution.py:46
  473.5 3.9 fusion.4
  477.3 0.0 all-reduce.14.cloned.1.call-update
  477.3 53.1 %all-reduce.14.cloned.1.call-done = f32[256,256]{1,0:T(8,128)} async-done(((f32[256,256]{1,0:T(8,128)}), f32[256,256]{1,0:T(8,128)}) %all-reduce.14.cloned.1.call-update) | async-done | bytes 262160 | tf_op jit(solution)/shard_map/psum | solution.py:47
  530.4 3.5 convolution_convert_fusion.1
  533.9 22.9 %subtract_convert_fusion = bf16[2560,5120]{1,0:T(8,128)(2,1)} fusion(bf16[2560,5120]{1,0:T(8,128)(2,1)} %param.4, bf16[2560,256]{1,0:T(8,128)(2,1)} %convolution_convert_fusion.1, bf16[128,5120]{1,0:T(8,128)(2,1)} %copy-done.5, bf16[128,5120]{1,0:T(8,128)(2,1)} %get-tuple-element.51), kind=kOutput, calls=%fused_computation.4 | convolution fusion | flops 6755450880 | bytes 56360960 | tf_op jit(solution)/shard_map/dot_general | solution.py:55
  556.8 0.7 broadcast_multiply_fusion
  (34 shorter events, 0.4 us)
Async XLA Ops:
  7.2 1.7 copy-start
  7.2 122.2 %all-reduce.8.cloned.1.call-start = ((), (), s32[]{:S(2)}) async-start(), calls=%async_computation | async-start | bytes 5242880 | tf_op jit(solution)/shard_map/psum | solution.py:36
  22.4 1.3 copy-start.10
  22.5 208.9 %all-reduce.16.cloned.1.call-start = ((), (), s32[]{:S(2)}) async-start(), calls=%async_computation.4 | async-start | bytes 11010048 | tf_op jit(solution)/shard_map/psum | solution.py:40
  136.9 143.4 %all-reduce.10.cloned.1.call-start = ((), (), s32[]{:S(2)}) async-start(), calls=%async_computation.1 | async-start | bytes 524288 | tf_op jit(solution)/shard_map/psum | solution.py:42
  231.4 13.7 %copy-start.6 = (f32[256,256]{0,1:T(8,128)S(1)}, f32[256,256]{0,1:T(8,128)}, u32[]{:S(2)}) copy-start(f32[256,256]{0,1:T(8,128)} %get-tuple-element.36) | copy-start | bytes 786436
  244.6 228.9 %all-reduce.12.cloned.1.call-start = ((), (), s32[]{:S(2)}) async-start(), calls=%async_computation.2 | async-start | bytes 5242880 | tf_op jit(solution)/shard_map/psum | solution.py:46
  342.2 5.4 copy-start.2
  352.1 3.5 copy-start.4
  354.5 1.1 copy-start.5
  355.6 13.8 %copy-start.9 = (f32[1,128,128]{1,2,0:T(8,128)S(1)}, f32[1,128,128]{1,2,0:T(8,128)}, u32[]{:S(2)}) copy-start(f32[1,128,128]{1,2,0:T(8,128)} %custom-call.19) | copy-start | bytes 196612
  369.3 38.6 %copy-start.3 = (f32[2560,256]{1,0:T(8,128)S(1)}, f32[2560,256]{1,0:T(8,128)}, u32[]{:S(2)}) copy-start(f32[2560,256]{1,0:T(8,128)} %all-reduce.8.cloned.1.call-done) | copy-start | bytes 7864324
  369.3 161.1 %all-reduce.14.cloned.1.call-start = ((), (), s32[]{:S(2)}) async-start(), calls=%async_computation.3 | async-start | bytes 524288 | tf_op jit(solution)/shard_map/psum | solution.py:47
  410.0 2.2 copy-start.8
  533.9 22.9 %copy-start.7 = (f32[256,256]{1,0:T(8,128)S(1)}, f32[256,256]{1,0:T(8,128)}, u32[]{:S(2)}) copy-start(f32[256,256]{1,0:T(8,128)} %all-reduce.14.cloned.1.call-done) | copy-start | bytes 786436
  533.9 23.6 %copy-start.1 = (bf16[5120,256]{1,0:T(8,128)(2,1)S(1)}, bf16[5120,256]{1,0:T(8,128)(2,1)}, u32[]{:S(2)}) copy-start(bf16[5120,256]{1,0:T(8,128)(2,1)} %param.5) | copy-start | bytes 7864324
Sparse Core Ops, SparseCore 0:
  22.6 106.7 all-reduce.7
  137.1 94.2 all-reduce.15
  244.7 35.6 all-reduce.9
  369.4 103.9 all-reduce.11
  477.5 52.9 all-reduce.13
where the time goes:
time: 573 us; the launch traced here: 565 us
  waiting for transfers between devices  311 us (54%)
  matrix products  112 us (20%)
  other arithmetic  110 us (19%)
  between operations  17 us (3%)
  local copies, waits for them, and re-layouts  13.1 us (2%)
    psum x1, waiting for transfers between devices, body(): sketch_cols = lax.psum(sketch_cols, 'row')  94.2 us
    psum x1, waiting for transfers between devices, body(): sketch_rows = lax.psum(sketch_rows, 'col')  90.6 us
    another operation x12, other arithmetic, orthonormal(): lower_factor = jnp.linalg.cholesky(gram_total)  68.7 us
    psum x1, waiting for transfers between devices, body(): applied = lax.psum(applied, 'col')  59.9 us
    psum x1, waiting for transfers between devices, body(): core_matrix = lax.psum(core_part(basis_rows, applied), 'row')  53.1 us
    another operation x5, other arithmetic, orthonormal(): jax.scipy.linalg.solve_triangular(lower_factor, sketch.T, lower=True)  40 us
    dot_general x1, matrix products, body(): lax.dot_general(projected, basis_cols, (((1,), (1,)), ((), ())), preferre...  22.9 us
    dot_general x2, matrix products, gram_matrix(): lax.dot_general(sketch, sketch, (((0,), (0,)), ((), ())), precision=lax.P...  20.6 us
  transfers between devices with their start and end apart: 5, of which 5 were waited for; matrix products, arithmetic and copies ran while one was open for 14% of the time, Pallas kernels for 0%

commit v1 on v0

v1 whole, which is shorter than its diff:
```python
import functools

import jax
import jax.numpy as jnp
from jax import lax
from jax.experimental import pallas as pl
from jax.experimental.pallas import tpu as pltpu
from jax.sharding import PartitionSpec as P

F32 = jnp.float32
BF16 = jnp.bfloat16
BASE = 64


def mm(a, b, dims=((1,), (0,))):
    return lax.dot_general(
        a, b, (dims, ((), ())), precision=lax.Precision.HIGHEST, preferred_element_type=F32
    )


def base_inverse(grams):
    size = grams[0].shape[0]
    tall = size // 8
    width = 2 * size
    eye = (
        lax.broadcasted_iota(jnp.int32, (size, size), 0) == lax.broadcasted_iota(jnp.int32, (size, size), 1)
    ).astype(F32)
    wide = [jnp.concatenate([g, eye], axis=1) for g in grams]
    parts = [[w[8 * t : 8 * t + 8] for t in range(tall)] for w in wide]
    sub = lax.broadcasted_iota(jnp.int32, (8, width), 0)
    for k in range(size):
        top, at = k // 8, k % 8
        for part in parts:
            row = part[top][at : at + 1, :]
            scaled = row * (1.0 / row[:, k : k + 1])
            for t in range(top, tall):
                col = part[t][:, k : k + 1]
                if t == top:
                    if at == 7:
                        continue
                    part[t] = part[t] - jnp.where(sub > at, col * scaled, 0.0)
                else:
                    part[t] = part[t] - col * scaled
    out = []
    for part in parts:
        full = jnp.concatenate(part, axis=0)
        left, right = full[:, :size], full[:, size:]
        pivot = jnp.sum(left * eye, axis=1, keepdims=True)
        out.append(right * lax.rsqrt(pivot))
    return out


def inverse_factors(grams):
    size = grams[0].shape[0]
    if size <= BASE:
        return base_inverse(grams)
    half = size // 2
    first = inverse_factors([g[:half, :half] for g in grams])
    lower = [mm(g[half:, :half], w, ((1,), (1,))) for g, w in zip(grams, first)]
    rest = [g[half:, half:] - mm(l, l, ((1,), (1,))) for g, l in zip(grams, lower)]
    second = inverse_factors(rest)
    out = []
    for w1, l21, w2 in zip(first, lower, second):
        below = -mm(w2, mm(l21, w1))
        out.append(
            jnp.concatenate(
                [
                    jnp.concatenate([w1, jnp.zeros_like(w1)], axis=1),
                    jnp.concatenate([below, w2], axis=1),
                ],
                axis=0,
            )
        )
    return out


def factor_kernel(order, total_ref, core_ref, middle_ref):
    w_r, w_c = inverse_factors([total_ref[0], total_ref[1]])
    core = mm(mm(w_r, total_ref[2]), w_c, ((1,), (1,)))
    core_ref[...] = core / jnp.sqrt(F32(order))
    middle_ref[...] = mm(mm(w_r, core, ((0,), (0,))), w_c)


def factor(total, order):
    size = total.shape[-1]
    shape = jax.ShapeDtypeStruct((size, size), F32)
    return pl.pallas_call(
        functools.partial(factor_kernel, order),
        out_shape=(shape, shape),
        in_specs=[pl.BlockSpec(memory_space=pltpu.VMEM)],
        out_specs=(pl.BlockSpec(memory_space=pltpu.VMEM),) * 2,
    )(total)


def split(x):
    high = x.astype(BF16)
    return high, (x - high.astype(F32)).astype(BF16)


def dot(a, b, dims=((1,), (0,))):
    return lax.dot_general(a, b, (dims, ((), ())), preferred_element_type=F32)


def body(order, front, right, left):
    y_part = lax.psum_scatter(dot(front, right), "col", tiled=True).astype(BF16)
    z_part = lax.psum_scatter(dot(front, left, ((0,), (0,))), "row", tiled=True).astype(BF16)
    y = lax.all_gather(y_part, "col", tiled=True)
    z = lax.all_gather(z_part, "row", tiled=True)
    high, low = split(dot(front, z))
    partial = jnp.stack(
        [
            dot(y_part, y_part, ((0,), (0,))),
            dot(z_part, z_part, ((0,), (0,))),
            dot(y, high, ((0,), (0,))) + dot(y, low, ((0,), (0,))),
        ]
    )
    total = lax.psum(partial, ("row", "col"))
    core_scaled, middle = factor(total, order)
    high, low = split(middle)
    projected = (dot(y, high) + dot(y, low)).astype(BF16)
    update = dot(projected, z, ((1,), (1,)))
    residual = (front.astype(F32) - update).astype(BF16)
    return residual, core_scaled


def solution(mesh):
    in_specs = (P("row", "col"), P("col", None), P("row", None))
    out_specs = (P("row", "col"), P())

    def run(front, right, left):
        inner = functools.partial(body, front.shape[0])
        return jax.shard_map(inner, mesh=mesh, in_specs=in_specs, out_specs=out_specs, check_vma=False)(
            front, right, left
        )

    return run
```

time: 573 us -> 395 us (0.69); the launches traced: 565 us -> 395 us
  other arithmetic: 110 us -> 3.89 us
  matrix products: 112 us -> 70.7 us
  waiting for transfers between devices: 311 us -> 277 us
  Pallas kernels: 0 us -> 28.1 us
  local copies, waits for them, and re-layouts: 13.1 us -> 0.86 us
    psum x5 -> x1, waiting for transfers between devices: 311 us -> 129 us  [body(): total = lax.psum(partial, ('row', 'col'))]
    another operation x17 -> x1, other arithmetic: 109 us -> 0.93 us  [body(): jnp.stack([dot(y_part, y_part, ((0,), (0,))), dot(z_part, z_part, ((0,),...]
    reduce_scatter x0 -> x2, waiting for transfers between devices: none -> 98.2 us  [the longest x1 52.7 us: body(): y_part = lax.psum_scatter(dot(front, right), 'col', tiled=True).astype(BF16)]
    all_gather x0 -> x2, waiting for transfers between devices: none -> 49.7 us  [the longest x1 29.8 us: body(): z = lax.all_gather(z_part, 'row', tiled=True)]
    pallas_call x0 -> x1, Pallas kernels: none -> 28.1 us  [factor(): pl.pallas_call(functools.partial(factor_kernel, order), out_shape=(shape,...]
    dot_general x8 -> x9, matrix products: 93.2 us -> 70.7 us  [dot(): return lax.dot_general(a, b, (dims, ((), ())), preferred_element_type=F32)]
    another operation x10 -> x0, matrix products: 18.8 us -> none  [the longest x6 17.9 us: orthonormal(): jax.scipy.linalg.solve_triangular(lower_factor, sketch.T, lower=True)]
    another operation x17 -> x0, local copies, waits for them, and re-layouts: 7.86 us -> none
  transfers between devices with their start and end apart: 5 -> 5, of which waited for: 5 -> 5; matrix products, arithmetic and copies ran while one was open for 14% -> 8% of each run, Pallas kernels for 0% -> 0%
where the time goes in v1:
time: 395 us
  waiting for transfers between devices  277 us (70%)
  matrix products  70.7 us (18%)
  Pallas kernels  28.1 us (7%)
  between operations  13.9 us (4%)
    psum x1, waiting for transfers between devices, body(): total = lax.psum(partial, ('row', 'col'))  129 us
    dot_general x9, matrix products, dot(): return lax.dot_general(a, b, (dims, ((), ())), preferred_element_type=F32)  70.7 us
    reduce_scatter x1, waiting for transfers between devices, body(): y_part = lax.psum_scatter(dot(front, right), 'col', tiled=True).astype(BF16)  52.7 us
    reduce_scatter x1, waiting for transfers between devices, body(): lax.psum_scatter(dot(front, left, ((0,), (0,))), 'row', tiled=True)  45.5 us
    all_gather x1, waiting for transfers between devices, body(): z = lax.all_gather(z_part, 'row', tiled=True)  29.8 us
    pallas_call x1, Pallas kernels, factor(): pl.pallas_call(functools.partial(factor_kernel, order), out_shape=(shape,...  28.1 us
    all_gather x1, waiting for transfers between devices, body(): y = lax.all_gather(y_part, 'col', tiled=True)  19.9 us
  transfers between devices with their start and end apart: 5, of which 5 were waited for; matrix products, arithmetic and copies ran while one was open for 8% of the time, Pallas kernels for 0%

profile of v1, /device:TPU:0, one launch (start us, length us, event | category | flops | bytes accessed | tf_op | source)
XLA Modules:
  0.0 394.7 jit_solution(7137516433033178815)
XLA Ops:
  7.2 0.0 copy-start
  7.2 0.0 reduce-scatter.5.cloned.1.call-start
  7.2 14.1 %fusion.10 = f32[5120,256]{1,0:T(8,128)} fusion(bf16[2560,5120]{1,0:T(8,128)(2,1)} %param.3, bf16[2560,256]{1,0:T(8,128)(2,1)} %param.5), kind=kOutput, calls=%fused_computation.18 | convolution fusion | flops 6710886400 | bytes 32768000 | tf_op jit(solution)/shard_map/dot_general | solution.py:101
  21.3 0.0 reduce-scatter.5.cloned.1.call-update
  21.4 0.0 reduce-scatter.3.cloned.1.call-start
  21.4 0.0 copy-done
  21.4 13.8 %fusion.9 = f32[2560,256]{1,0:T(8,128)} fusion(bf16[2560,5120]{1,0:T(8,128)(2,1)} %param.3, bf16[5120,256]{1,0:T(8,128)(2,1)S(1)} %copy-done), kind=kOutput, calls=%fused_computation.17 | convolution fusion | flops 6710886400 | bytes 31457280 | tf_op jit(solution)/shard_map/dot_general | solution.py:101
  35.2 0.0 reduce-scatter.3.cloned.1.call-update
  35.2 0.0 all-gather.5.cloned.1.call-start
  35.2 45.5 %reduce-scatter.5.cloned.1.call-done = f32[640,256]{1,0:T(8,128)} async-done(((f32[5120,256]{1,0:T(8,128)}), f32[640,256]{1,0:T(8,128)}) %reduce-scatter.5.cloned.1.call-update) | async-done | bytes 655376 | tf_op jit(solution)/shard_map/reduce_scatter | solution.py:106
  80.7 1.8 convert_element_type.35
  82.6 0.0 copy-start.4
  82.6 0.0 all-gather.5.cloned.1.call-update
  82.6 0.0 all-gather.3.cloned.1.call-start
  82.7 52.7 %reduce-scatter.3.cloned.1.call-done = f32[640,256]{1,0:T(8,128)} async-done(((f32[2560,256]{1,0:T(8,128)}), f32[640,256]{1,0:T(8,128)}) %reduce-scatter.3.cloned.1.call-update) | async-done | bytes 655376 | tf_op jit(solution)/shard_map/reduce_scatter | solution.py:105
  135.3 1.1 convert_element_type.34
  136.4 0.0 copy-start.5
  136.5 0.3 convolution_bitcast_fusion.2
  136.8 0.4 copy-done.5
  137.2 0.0 all-gather.3.cloned.1.call-update
  137.2 0.0 all-reduce.2.cloned.1.call-start
  137.3 0.0 copy-done.4
  137.3 0.3 convolution_bitcast_fusion.1
  137.6 29.8 %all-gather.5.cloned.1.call-done = bf16[5120,256]{1,0:T(8,128)(2,1)} async-done(((bf16[640,256]{1,0:T(8,128)(2,1)}), bf16[5120,256]{1,0:T(8,128)(2,1)}) %all-gather.5.cloned.1.call-update) | async-done | bytes 2621456 | tf_op jit(solution)/shard_map/all_gather | solution.py:108
  167.4 14.1 %convolution_bitcast_fusion = f32[2560,256]{0,1:T(8,128)} fusion(bf16[5120,256]{1,0:T(8,128)(2,1)} %all-gather.5.cloned.1.call-done, bf16[2560,5120]{1,0:T(8,128)(2,1)} %param.3), kind=kOutput, calls=%fused_computation.2 | convolution fusion | flops 6710886400 | bytes 31457280 | tf_op jit(solution)/shard_map/dot_general | solution.py:101
  181.4 19.9 %all-gather.3.cloned.1.call-done = bf16[2560,256]{1,0:T(8,128)(2,1)} async-done(((bf16[640,256]{1,0:T(8,128)(2,1)}), bf16[2560,256]{1,0:T(8,128)(2,1)}) %all-gather.3.cloned.1.call-update) | async-done | bytes 1310736 | tf_op jit(solution)/shard_map/all_gather | solution.py:107
  201.3 0.0 copy-start.2
  201.3 0.0 copy-start.3
  201.3 3.6 fusion.1
  205.0 0.0 copy-done.2
  205.0 0.4 copy-done.3
  205.4 0.6 fusion.2
  206.0 0.9 pad_maximum_fusion
  206.9 0.0 all-reduce.2.cloned.1.call-update
  207.0 129.1 %all-reduce.2.cloned.1.call-done.total_ref = f32[3,256,256]{2,1,0:T(8,128)} async-done(((f32[3,256,256]{2,1,0:T(8,128)}), f32[3,256,256]{2,1,0:T(8,128)}) %all-reduce.2.cloned.1.call-update) | async-done | bytes 786448 | tf_op jit(solution)/shard_map/psum | solution.py:117
  336.1 28.1 %shard_map.50 = (f32[256,256]{1,0:T(8,128)}, f32[256,256]{1,0:T(8,128)}) custom-call(f32[3,256,256]{2,1,0:T(8,128)} %all-reduce.2.cloned.1.call-done.total_ref), custom_call_target="tpu_custom_call" | custom-call | tf_op jit(solution)/shard_map/pallas_call | solution.py:87
  364.2 0.0 copy-start.6
  364.2 3.0 fusion.7
  367.2 0.0 copy-done.6
  367.2 0.0 copy-start.1
  367.2 20.9 %subtract_convert_fusion = bf16[2560,5120]{1,0:T(8,128)(2,1)} fusion(bf16[2560,5120]{1,0:T(8,128)(2,1)} %param.3, bf16[5120,256]{1,0:T(8,128)(2,1)} %all-gather.5.cloned.1.call-done, f32[2560,256]{1,0:T(8,128)} %fusion.7, bf16[2560,256]{1,0:T(8,128)(2,1)} %all-gather.3.cloned.1.call-done, f32[256,256]{1,0:T(8,128)S(1)} %copy-done.6), kind=kOutput, calls=%fused_computation | convolution fusion | flops 7087325184 | bytes 59244544 | tf_op jit(solution)/shard_map/dot_general | solution.py:101
  388.1 0.0 copy-done.1
Async XLA Ops:
  7.2 14.2 %copy-start = (bf16[5120,256]{1,0:T(8,128)(2,1)S(1)}, bf16[5120,256]{1,0:T(8,128)(2,1)}, u32[]{:S(2)}) copy-start(bf16[5120,256]{1,0:T(8,128)(2,1)} %param.4) | copy-start | bytes 7864324
  7.2 73.6 %reduce-scatter.5.cloned.1.call-start = ((), (), s32[]{:S(2)}) async-start(), calls=%async_computation.4 | async-start | bytes 5898240 | tf_op jit(solution)/shard_map/reduce_scatter | solution.py:106
  21.4 114.0 %reduce-scatter.3.cloned.1.call-start = ((), (), s32[]{:S(2)}) async-start(), calls=%async_computation.2 | async-start | bytes 3276800 | tf_op jit(solution)/shard_map/reduce_scatter | solution.py:105
  35.2 132.2 %all-gather.5.cloned.1.call-start = ((), (), s32[]{:S(2)}) async-start(), calls=%async_computation.5 | async-start | bytes 2949120 | tf_op jit(solution)/shard_map/all_gather | solution.py:108
  82.6 54.7 %copy-start.4 = (bf16[640,256]{1,0:T(8,128)(2,1)S(1)}, bf16[640,256]{1,0:T(8,128)(2,1)}, u32[]{:S(2)}) copy-start(bf16[640,256]{1,0:T(8,128)(2,1)} %convert_element_type.35) | copy-start | bytes 983044
  82.6 118.7 %all-gather.3.cloned.1.call-start = ((), (), s32[]{:S(2)}) async-start(), calls=%async_computation.3 | async-start | bytes 1638400 | tf_op jit(solution)/shard_map/all_gather | solution.py:107
  136.4 0.7 copy-start.5
  137.2 198.9 %all-reduce.2.cloned.1.call-start = ((), (), s32[]{:S(2)}) async-start(), calls=%async_computation.6 | async-start | bytes 1572864 | tf_op jit(solution)/shard_map/psum | solution.py:117
  201.3 3.7 copy-start.2
  201.3 4.1 %copy-start.3 = (f32[2560,256]{0,1:T(8,128)S(1)}, f32[2560,256]{0,1:T(8,128)}, u32[]{:S(2)}) copy-start(f32[2560,256]{0,1:T(8,128)} %convolution_bitcast_fusion) | copy-start | bytes 7864324
  364.2 3.0 copy-start.6
  367.2 20.9 %copy-start.1 = (bf16[5120,256]{1,0:T(8,128)(2,1)S(1)}, bf16[5120,256]{1,0:T(8,128)(2,1)}, u32[]{:S(2)}) copy-start(bf16[5120,256]{1,0:T(8,128)(2,1)} %param.4) | copy-start | bytes 7864324
Sparse Core Ops, SparseCore 0:
  21.5 59.2 reduce-scatter.4
  83.0 52.2 reduce-scatter.2
  137.8 29.5 all-gather.4
  168.8 32.5 all-gather.2
  207.1 128.9 all-reduce.1

commit v2 on v1

--- a/solution.py
+++ b/solution.py
@@ -75,8 +75,10 @@
 
 
 def factor_kernel(order, total_ref, core_ref, middle_ref):
-    w_r, w_c = inverse_factors([total_ref[0], total_ref[1]])
-    core = mm(mm(w_r, total_ref[2]), w_c, ((1,), (1,)))
+    size = core_ref.shape[0]
+    gram_r, cross, gram_c = (total_ref[:, n].reshape(size, size) for n in range(3))
+    w_r, w_c = inverse_factors([gram_r, gram_c])
+    core = mm(mm(w_r, cross), w_c, ((1,), (1,)))
     core_ref[...] = core / jnp.sqrt(F32(order))
     middle_ref[...] = mm(mm(w_r, core, ((0,), (0,))), w_c)
 
@@ -101,21 +103,165 @@
     return lax.dot_general(a, b, (dims, ((), ())), preferred_element_type=F32)
 
 
-def body(order, front, right, left):
-    y_part = lax.psum_scatter(dot(front, right), "col", tiled=True).astype(BF16)
-    z_part = lax.psum_scatter(dot(front, left, ((0,), (0,))), "row", tiled=True).astype(BF16)
-    y = lax.all_gather(y_part, "col", tiled=True)
-    z = lax.all_gather(z_part, "row", tiled=True)
+def greet(groups):
+    barrier = pltpu.get_barrier_semaphore()
+    for axis, count in groups:
+        me = lax.axis_index(axis)
+        for step in range(1, count):
+            pl.semaphore_signal(
+                barrier, inc=1, device_id={axis: lax.rem(me + step, count)}, device_id_type=pl.DeviceIdType.MESH
+            )
+    pl.semaphore_wait(barrier, sum(count - 1 for _, count in groups))
+
+
+def scatter(axis, count, source, slots, send, recv):
+    me = lax.axis_index(axis)
+    copies = []
+    for step in range(1, count):
+        peer = lax.rem(me + step, count)
+        copies.append(
+            pltpu.make_async_remote_copy(
+                src_ref=source(peer),
+                dst_ref=slots.at[step - 1],
+                send_sem=send.at[step - 1],
+                recv_sem=recv.at[step - 1],
+                device_id={axis: peer},
+                device_id_type=pl.DeviceIdType.MESH,
+            )
+        )
+    for copy in copies:
+        copy.start()
+    return copies
+
+
+def gather(axis, count, blocks, send, recv):
+    me = lax.axis_index(axis)
+    sends, receives = [], []
+    for step in range(1, count):
+        for slot, peer, bag in (
+            (me, lax.rem(me + step, count), sends),
+            (lax.rem(me - step + count, count), lax.rem(me + step, count), receives),
+        ):
+            bag.append(
+                pltpu.make_async_remote_copy(
+                    src_ref=blocks.at[me],
+                    dst_ref=blocks.at[slot],
+                    send_sem=send.at[step - 1],
+                    recv_sem=recv.at[step - 1],
+                    device_id={axis: peer},
+                    device_id_type=pl.DeviceIdType.MESH,
+                )
+            )
+    for copy in sends:
+        copy.start()
+    return sends, receives
+
+
+def finish(pair):
+    for copy in pair[1]:
+        copy.wait_recv()
+    for copy in pair[0]:
+        copy.wait_send()
+
+
+def share_kernel(rows, cols, yp_ref, zp_ref, y_ref, z_ref, y_buf, z_buf, *sems):
+    greet((("row", rows), ("col", cols)))
+    me_r, me_c = lax.axis_index("row"), lax.axis_index("col")
+    z_in = scatter("row", rows, lambda k: zp_ref.at[k], z_buf, sems[0], sems[1])
+    y_in = scatter("col", cols, lambda k: yp_ref.at[k], y_buf, sems[2], sems[3])
+    for copy in z_in:
+        copy.wait()
+    total = zp_ref[me_r].astype(F32)
+    for step in range(rows - 1):
+        total = total + z_buf[step].astype(F32)
+    z_ref[me_r] = total.astype(BF16)
+    z_out = gather("row", rows, z_ref, sems[4], sems[5])
+    for copy in y_in:
+        copy.wait()
+    total = yp_ref[me_c]
+    for step in range(cols - 1):
+        total = total + y_buf[step]
+    y_ref[me_c] = total.astype(BF16)
+    y_out = gather("col", cols, y_ref, sems[6], sems[7])
+    finish(z_out)
+    finish(y_out)
+
+
+def share(yp, zp):
+    cols, y_rows, size = yp.shape
+    rows, z_rows, _ = zp.shape
+    dma = pltpu.SemaphoreType.DMA
+    return pl.pallas_call(
+        functools.partial(share_kernel, rows, cols),
+        out_shape=(jax.ShapeDtypeStruct(yp.shape, BF16), jax.ShapeDtypeStruct(zp.shape, BF16)),
+        in_specs=[pl.BlockSpec(memory_space=pltpu.VMEM)] * 2,
+        out_specs=(pl.BlockSpec(memory_space=pltpu.VMEM),) * 2,
+        scratch_shapes=[
+            pltpu.VMEM((cols - 1, y_rows, size), F32),
+            pltpu.VMEM((rows - 1, z_rows, size), BF16),
+        ]
+        + [dma((n - 1,)) for n in (rows, rows, cols, cols, rows, rows, cols, cols)],
+        compiler_params=pltpu.CompilerParams(collective_id=0, has_side_effects=True),
+    )(yp, zp)
+
+
+def total_kernel(rows, cols, both_ref, gram_ref, total_ref, row_buf, own, col_buf, *sems):
+    greet((("row", rows), ("col", cols)))
+    me_r, me_c = lax.axis_index("row"), lax.axis_index("col")
+    height = gram_ref.shape[0]
+
+    def piece(k):
+        return both_ref.at[:, pl.ds(pl.multiple_of(k * height, 8), height), :]
+
+    for copy in scatter("row", rows, piece, row_buf, sems[0], sems[1]):
+        copy.wait()
+    summed = piece(me_r)[...]
+    for step in range(rows - 1):
+        summed = summed + row_buf[step]
+    total_ref[me_r, 0] = summed[0]
+    own[0] = summed[1]
+    own[1] = gram_ref[...]
+    col_buf[cols - 1] = own[...]
+    for copy in scatter("col", cols, lambda k: own, col_buf, sems[2], sems[3]):
+        copy.wait()
+    summed = None
+    for member in range(cols):
+        slot = lax.rem(me_c - member + 2 * cols - 1, cols)
+        summed = col_buf[slot] if summed is None else summed + col_buf[slot]
+    total_ref[me_r, 1] = summed[0]
+    total_ref[me_r, 2] = summed[1]
+    finish(gather("row", rows, total_ref, sems[4], sems[5]))
+
+
+def total_of(both, gram, rows, cols):
+    height, size = gram.shape
+    dma = pltpu.SemaphoreType.DMA
+    return pl.pallas_call(
+        functools.partial(total_kernel, rows, cols),
+        out_shape=jax.ShapeDtypeStruct((rows, 3, height, size), F32),
+        in_specs=[pl.BlockSpec(memory_space=pltpu.VMEM)] * 2,
+        out_specs=pl.BlockSpec(memory_space=pltpu.VMEM),
+        scratch_shapes=[
+            pltpu.VMEM((rows - 1, 2, height, size), F32),
+            pltpu.VMEM((2, height, size), F32),
+            pltpu.VMEM((cols, 2, height, size), F32),
+        ]
+        + [dma((n - 1,)) for n in (rows, rows, cols, cols, rows, rows)],
+        compiler_params=pltpu.CompilerParams(collective_id=1, has_side_effects=True),
+    )(both, gram)
+
+
+def body(order, rows, cols, front, right, left):
+    size = right.shape[1]
+    yp = dot(front, right).reshape(cols, -1, size)
+    zp = dot(front, left, ((0,), (0,))).astype(BF16).reshape(rows, -1, size)
+    y, z = share(yp, zp)
+    y, z = y.reshape(-1, size), z.reshape(-1, size)
     high, low = split(dot(front, z))
-    partial = jnp.stack(
-        [
-            dot(y_part, y_part, ((0,), (0,))),
-            dot(z_part, z_part, ((0,), (0,))),
-            dot(y, high, ((0,), (0,))) + dot(y, low, ((0,), (0,))),
-        ]
-    )
-    total = lax.psum(partial, ("row", "col"))
-    core_scaled, middle = factor(total, order)
+    both = jnp.stack([dot(y, y, ((0,), (0,))), dot(y, high, ((0,), (0,))) + dot(y, low, ((0,), (0,)))])
+    height = size // rows
+    gram = lax.dynamic_slice_in_dim(dot(z, z, ((0,), (0,))), lax.axis_index("row") * height, height)
+    core_scaled, middle = factor(total_of(both, gram, rows, cols), order)
     high, low = split(middle)
     projected = (dot(y, high) + dot(y, low)).astype(BF16)
     update = dot(projected, z, ((1,), (1,)))
@@ -128,7 +274,7 @@
     out_specs = (P("row", "col"), P())
 
     def run(front, right, left):
-        inner = functools.partial(body, front.shape[0])
+        inner = functools.partial(body, front.shape[0], mesh.shape["row"], mesh.shape["col"])
         return jax.shard_map(inner, mesh=mesh, in_specs=in_specs, out_specs=out_specs, check_vma=False)(
             front, right, left
         )

time: 395 us -> 236 us (0.60)
  waiting for transfers between devices: 277 us -> 0 us
  Pallas kernels: 28.1 us -> 158 us
  between operations: 13.9 us -> 0.71 us
    pallas_call x0 -> x2, Pallas kernels: none -> 130 us  [the longest x1 95.5 us: share(): pl.pallas_call(functools.partial(share_kernel, rows, cols), out_shape=(ja...]
    psum x1 -> x0, waiting for transfers between devices: 129 us -> none  [body(): total = lax.psum(partial, ('row', 'col'))]
    reduce_scatter x2 -> x0, waiting for transfers between devices: 98.2 us -> none  [the longest x1 52.7 us: body(): y_part = lax.psum_scatter(dot(front, right), 'col', tiled=True).astype(BF16)]
    all_gather x2 -> x0, waiting for transfers between devices: 49.7 us -> none  [the longest x1 29.8 us: body(): z = lax.all_gather(z_part, 'row', tiled=True)]
  transfers between devices with their start and end apart: 5 -> 0, of which waited for: 5 -> 0; matrix products, arithmetic and copies ran while one was open for 8% -> 0% of each run, Pallas kernels for 0% -> 0%
where the time goes in v2:
time: 236 us; the launch traced here: 235 us
  Pallas kernels  158 us (67%)
  matrix products  72.7 us (31%)
  local copies, waits for them, and re-layouts  2.53 us (1%)
    pallas_call x1, Pallas kernels, share(): pl.pallas_call(functools.partial(share_kernel, rows, cols), out_shape=(ja...  95.5 us
    dot_general x9, matrix products, dot(): return lax.dot_general(a, b, (dims, ((), ())), preferred_element_type=F32)  72.7 us
    pallas_call x1, Pallas kernels, total_of(): pl.pallas_call(functools.partial(total_kernel, rows, cols), out_shape=jax...  34.7 us
    pallas_call x1, Pallas kernels, factor(): pl.pallas_call(functools.partial(factor_kernel, order), out_shape=(shape,...  28.1 us

profile of v2, /device:TPU:0, one launch (start us, length us, event | category | flops | bytes accessed | tf_op | source)
XLA Modules:
  0.0 235.0 jit_solution(1713958725147604519)
XLA Ops:
  0.6 0.0 copy-start
  0.7 1.7 copy-done
  2.4 0.0 copy-start.6
  2.4 13.6 %fusion.9 = f32[2560,256]{1,0:T(8,128)} fusion(bf16[2560,5120]{1,0:T(8,128)(2,1)} %param.3, bf16[5120,256]{1,0:T(8,128)(2,1)S(1)} %copy-done), kind=kOutput, calls=%fused_computation.19 | convolution fusion | flops 6710886400 | bytes 31457280 | tf_op jit(solution)/shard_map/dot_general | solution.py:103
  16.0 0.0 copy-done.6
  16.0 14.0 %convolution_convert_fusion = bf16[5120,256]{1,0:T(8,128)(2,1)} fusion(bf16[2560,5120]{1,0:T(8,128)(2,1)} %param.3, bf16[2560,256]{1,0:T(8,128)(2,1)S(1)} %copy-done.6), kind=kOutput, calls=%fused_computation.1 | convolution fusion | flops 6712197120 | bytes 30146560 | tf_op jit(solution)/shard_map/dot_general | solution.py:103
  30.0 95.5 %shard_map.50 = (bf16[4,640,256]{2,1,0:T(8,128)(2,1)}, bf16[8,640,256]{2,1,0:T(8,128)(2,1)}) custom-call(f32[4,640,256]{2,1,0:T(8,128)} %bitcast.34, bf16[8,640,256]{2,1,0:T(8,128)(2,1)} %bitcast.35), custom_call_target="tpu_custom_call" | custom-call | tf_op jit(solution)/shard_map/pallas_call | solution.py:194
  125.5 0.0 copy-start.5
  125.6 2.4 %convolution_bitcast_fusion.2 = f32[1,256,256]{2,1,0:T(8,128)S(1)} fusion(bf16[4,640,256]{2,1,0:T(8,128)(2,1)} %get-tuple-element.6), kind=kOutput, calls=%fused_computation.10 | convolution fusion | flops 335544320 | bytes 1572864 | tf_op jit(solution)/shard_map/dot_general | solution.py:103
  128.0 0.1 copy-done.5
  128.1 0.9 convolution_bitcast_fusion.1
  129.0 0.6 constant_dynamic-slice_fusion.gram_ref
  129.6 0.0 copy-start.2
  129.6 14.0 %convolution_bitcast_fusion = f32[2560,256]{0,1:T(8,128)} fusion(bf16[5120,256]{1,0:T(8,128)(2,1)} %bitcast.32, bf16[2560,5120]{1,0:T(8,128)(2,1)} %param.3), kind=kOutput, calls=%fused_computation.3 | convolution fusion | flops 6710886400 | bytes 31457280 | tf_op jit(solution)/shard_map/dot_general | solution.py:103
  143.6 0.0 copy-done.2
  143.6 0.0 copy-start.3
  143.6 3.3 %fusion.1 = f32[256,256]{1,0:T(8,128)S(1)} fusion(bf16[2560,256]{1,0:T(8,128)(2,1)S(1)} %bitcast.29, f32[2560,256]{0,1:T(8,128)} %convolution_bitcast_fusion), kind=kOutput, calls=%fused_computation.6 | convolution fusion | flops 338165760 | bytes 4194304 | tf_op jit(solution)/shard_map/dot_general | solution.py:103
  146.8 0.0 copy-done.3
  146.9 0.6 fusion.2
  147.5 0.8 pad_maximum_fusion.both_ref
  148.3 34.7 %shard_map.51.total_ref = f32[8,3,32,256]{3,2,1,0:T(8,128)} custom-call(f32[2,256,256]{2,1,0:T(8,128)} %pad_maximum_fusion.both_ref, f32[32,256]{1,0:T(8,128)} %constant_dynamic-slice_fusion.gram_ref), custom_call_target="tpu_custom_call" | custom-call | tf_op jit(solution)/shard_map/pallas_call | solution.py:239
  183.0 28.1 %shard_map.52 = (f32[256,256]{1,0:T(8,128)}, f32[256,256]{1,0:T(8,128)}) custom-call(f32[8,3,32,256]{3,2,1,0:T(8,128)} %shard_map.51.total_ref), custom_call_target="tpu_custom_call" | custom-call | tf_op jit(solution)/shard_map/pallas_call | solution.py:89
  211.1 0.0 copy-start.4
  211.1 3.0 %fusion.7 = f32[2560,256]{1,0:T(8,128)} fusion(bf16[2560,256]{1,0:T(8,128)(2,1)S(1)} %bitcast.31, f32[256,256]{1,0:T(8,128)} %get-tuple-element.8), kind=kOutput, calls=%fused_computation.16 | convolution fusion | flops 335609856 | bytes 4194304 | tf_op jit(solution)/shard_map/dot_general | solution.py:103
  214.1 0.0 copy-done.4
  214.1 0.0 copy-start.1
  214.1 20.9 %subtract_convert_fusion = bf16[2560,5120]{1,0:T(8,128)(2,1)} fusion(bf16[2560,5120]{1,0:T(8,128)(2,1)} %param.3, bf16[5120,256]{1,0:T(8,128)(2,1)} %bitcast.33, f32[2560,256]{1,0:T(8,128)} %fusion.7, bf16[2560,256]{1,0:T(8,128)(2,1)} %bitcast.28, f32[256,256]{1,0:T(8,128)S(1)} %copy-done.4), kind=kOutput, calls=%fused_computation | convolution fusion | flops 7087325184 | bytes 59244544 | tf_op jit(solution)/shard_map/dot_general | solution.py:103
  235.0 0.0 copy-done.1
Async XLA Ops:
  0.6 1.7 copy-start
  2.4 13.6 %copy-start.6 = (bf16[2560,256]{1,0:T(8,128)(2,1)S(1)}, bf16[2560,256]{1,0:T(8,128)(2,1)}, u32[]{:S(2)}) copy-start(bf16[2560,256]{1,0:T(8,128)(2,1)} %param.5) | copy-start | bytes 3932164
  125.5 2.5 %copy-start.5 = (bf16[8,640,256]{2,1,0:T(8,128)(2,1)S(1)}, bf16[8,640,256]{2,1,0:T(8,128)(2,1)}, u32[]{:S(2)}) copy-start(bf16[8,640,256]{2,1,0:T(8,128)(2,1)} %get-tuple-element.7) | copy-start | bytes 7864324
  129.6 14.0 %copy-start.2 = (bf16[4,640,256]{2,1,0:T(8,128)(2,1)S(1)}, bf16[4,640,256]{2,1,0:T(8,128)(2,1)}, u32[]{:S(2)}) copy-start(bf16[4,640,256]{2,1,0:T(8,128)(2,1)} %get-tuple-element.6) | copy-start | bytes 3932164
  143.6 3.3 %copy-start.3 = (f32[2560,256]{0,1:T(8,128)S(1)}, f32[2560,256]{0,1:T(8,128)}, u32[]{:S(2)}) copy-start(f32[2560,256]{0,1:T(8,128)} %convolution_bitcast_fusion) | copy-start | bytes 7864324
  211.1 3.0 %copy-start.4 = (f32[256,256]{1,0:T(8,128)S(1)}, f32[256,256]{1,0:T(8,128)}, u32[]{:S(2)}) copy-start(f32[256,256]{1,0:T(8,128)} %get-tuple-element.8) | copy-start | bytes 786436
  214.1 20.9 %copy-start.1 = (bf16[5120,256]{1,0:T(8,128)(2,1)S(1)}, bf16[5120,256]{1,0:T(8,128)(2,1)}, u32[]{:S(2)}) copy-start(bf16[5120,256]{1,0:T(8,128)(2,1)} %param.4) | copy-start | bytes 7864324

commit v3 on v2

--- a/solution.py
+++ b/solution.py
@@ -1,4 +1,5 @@
 import functools
+import math
 
 import jax
 import jax.numpy as jnp
@@ -164,45 +165,173 @@
         copy.wait_send()
 
 
-def share_kernel(rows, cols, yp_ref, zp_ref, y_ref, z_ref, y_buf, z_buf, *sems):
+def hop(source, target, send, recv, peer):
+    return pltpu.make_async_remote_copy(
+        src_ref=source,
+        dst_ref=target,
+        send_sem=send,
+        recv_sem=recv,
+        device_id={"col": peer},
+        device_id_type=pl.DeviceIdType.MESH,
+    )
+
+
+def chain_step(step, cols, yp_ref, bufs, send, recv):
+    me = lax.axis_index("col")
+    for way in range(2):
+        place = me if way == 0 else cols - 1 - me
+        to = me + 1 if way == 0 else me - 1
+        far = cols - 1 - (step - place)
+        chunk = far if way == 0 else cols - 1 - far
+        buf, s_sem, r_sem = bufs[way], send.at[way, step], recv.at[way, step]
+
+        @pl.when(place == 0)
+        def _():
+            hop(yp_ref.at[chunk], buf.at[step], s_sem, r_sem, to).start()
+
+        if step > 0:
+
+            @pl.when((place >= 1) & (place <= step))
+            def _():
+                hop(buf.at[step - 1], buf.at[step - 1], send.at[way, step - 1], recv.at[way, step - 1], to).wait_recv()
+                buf[step - 1] = buf[step - 1] + yp_ref[chunk]
+                hop(buf.at[step - 1], buf.at[step], s_sem, r_sem, to).start()
+
+
+def chain_end(cols, yp_ref, y_ref, acc, bufs, send, recv):
+    me = lax.axis_index("col")
+    last = cols - 2
+    acc[...] = yp_ref[me]
+    for way in range(2):
+        place = me if way == 0 else cols - 1 - me
+        came = me - 1 if way == 0 else me + 1
+        buf = bufs[way]
+
+        @pl.when(place >= 1)
+        def _():
+            hop(buf.at[last], buf.at[last], send.at[way, last], recv.at[way, last], came).wait_recv()
+            acc[...] = acc[...] + buf[last]
+
+    y_ref[me] = acc[...].astype(BF16)
+    for way in range(2):
+        place = me if way == 0 else cols - 1 - me
+        to = me + 1 if way == 0 else me - 1
+        for step in range(cols - 1):
+
+            @pl.when(place <= step)
+            def _():
+                hop(acc, bufs[way].at[step], send.at[way, step], recv.at[way, step], to).wait_send()
+
+
+def spread(cols, y_ref, send, recv):
+    me = lax.axis_index("col")
+
+    def each(step, act):
+        for way in range(2):
+            place = me if way == 0 else cols - 1 - me
+            sign = 1 if way == 0 else -1
+            s_sem, r_sem = send.at[way, step], recv.at[way, step]
+            if act == "got":
+
+                @pl.when(place >= step + 1)
+                def _():
+                    block = y_ref.at[me - sign * (step + 1)]
+                    hop(block, block, s_sem, r_sem, me - sign).wait_recv()
+
+            else:
+
+                @pl.when((place >= step) & (place < cols - 1))
+                def _():
+                    block = y_ref.at[me - sign * step]
+                    copy = hop(block, block, s_sem, r_sem, me + sign)
+                    if act == "send":
+                        copy.start()
+                    else:
+                        copy.wait_send()
+
+    for step in range(cols - 1):
+        each(step, "send")
+        each(step, "got")
+    for step in range(cols - 1):
+        each(step, "sent")
+
+
+def share_kernel(
+    rows, cols, tile, yp_ref, left_ref, front_ref, y_ref, z_ref, zp, z_buf, right_buf, left_buf, acc, tiles, t_sem, *sems
+):
     greet((("row", rows), ("col", cols)))
-    me_r, me_c = lax.axis_index("row"), lax.axis_index("col")
-    z_in = scatter("row", rows, lambda k: zp_ref.at[k], z_buf, sems[0], sems[1])
-    y_in = scatter("col", cols, lambda k: yp_ref.at[k], y_buf, sems[2], sems[3])
+    me_r = lax.axis_index("row")
+    chain = (cols, yp_ref, (right_buf, left_buf), sems[2], sems[3])
+    z_rows, size = zp.shape[1:]
+    count = front_ref.shape[1] // tile
+    group = tile // z_rows
+
+    def fetch(t):
+        slot = lax.rem(t, 2)
+        return pltpu.make_async_copy(
+            front_ref.at[:, pl.ds(pl.multiple_of(t * tile, 128), tile)], tiles.at[slot], t_sem.at[slot]
+        )
+
+    chain_step(0, *chain)
+    fetch(0).start()
+
+    @pl.loop(0, count)
+    def _(t):
+        @pl.when(t + 1 < count)
+        def _():
+            fetch(t + 1).start()
+
+        fetch(t).wait()
+        part = dot(left_ref[...], tiles[lax.rem(t, 2)]).T.astype(BF16)
+        for n in range(group):
+            zp[t * group + n] = part[n * z_rows : (n + 1) * z_rows]
+
+    z_in = scatter("row", rows, lambda k: zp.at[k], z_buf, sems[0], sems[1])
+    for step in range(1, cols - 1):
+        chain_step(step, *chain)
     for copy in z_in:
         copy.wait()
-    total = zp_ref[me_r].astype(F32)
+    total = zp[me_r].astype(F32)
     for step in range(rows - 1):
         total = total + z_buf[step].astype(F32)
     z_ref[me_r] = total.astype(BF16)
     z_out = gather("row", rows, z_ref, sems[4], sems[5])
-    for copy in y_in:
-        copy.wait()
-    total = yp_ref[me_c]
-    for step in range(cols - 1):
-        total = total + y_buf[step]
-    y_ref[me_c] = total.astype(BF16)
-    y_out = gather("col", cols, y_ref, sems[6], sems[7])
+    chain_end(cols, yp_ref, y_ref, acc, (right_buf, left_buf), sems[2], sems[3])
+    spread(cols, y_ref, sems[6], sems[7])
     finish(z_out)
-    finish(y_out)
-
-
-def share(yp, zp):
+
+
+def share(yp, left, front, rows):
     cols, y_rows, size = yp.shape
-    rows, z_rows, _ = zp.shape
+    depth, width = front.shape
+    z_rows = width // rows
+    tile = z_rows * 128 // math.gcd(z_rows, 128)
     dma = pltpu.SemaphoreType.DMA
+    vmem = pl.BlockSpec(memory_space=pltpu.VMEM)
     return pl.pallas_call(
-        functools.partial(share_kernel, rows, cols),
-        out_shape=(jax.ShapeDtypeStruct(yp.shape, BF16), jax.ShapeDtypeStruct(zp.shape, BF16)),
-        in_specs=[pl.BlockSpec(memory_space=pltpu.VMEM)] * 2,
-        out_specs=(pl.BlockSpec(memory_space=pltpu.VMEM),) * 2,
+        functools.partial(share_kernel, rows, cols, tile),
+        out_shape=(jax.ShapeDtypeStruct(yp.shape, BF16), jax.ShapeDtypeStruct((rows, z_rows, size), BF16)),
+        in_specs=[vmem, vmem, pl.BlockSpec(memory_space=pl.ANY)],
+        out_specs=(vmem, vmem),
         scratch_shapes=[
+            pltpu.VMEM((rows, z_rows, size), BF16),
+            pltpu.VMEM((rows - 1, z_rows, size), BF16),
             pltpu.VMEM((cols - 1, y_rows, size), F32),
-            pltpu.VMEM((rows - 1, z_rows, size), BF16),
-        ]
-        + [dma((n - 1,)) for n in (rows, rows, cols, cols, rows, rows, cols, cols)],
+            pltpu.VMEM((cols - 1, y_rows, size), F32),
+            pltpu.VMEM((y_rows, size), F32),
+            pltpu.VMEM((2, depth, tile), BF16),
+            dma((2,)),
+            dma((rows - 1,)),
+            dma((rows - 1,)),
+            dma((2, cols - 1)),
+            dma((2, cols - 1)),
+            dma((rows - 1,)),
+            dma((rows - 1,)),
+            dma((2, cols - 1)),
+            dma((2, cols - 1)),
+        ],
         compiler_params=pltpu.CompilerParams(collective_id=0, has_side_effects=True),
-    )(yp, zp)
+    )(yp, left, front)
 
 
 def total_kernel(rows, cols, both_ref, gram_ref, total_ref, row_buf, own, col_buf, *sems):
@@ -254,8 +383,7 @@
 def body(order, rows, cols, front, right, left):
     size = right.shape[1]
     yp = dot(front, right).reshape(cols, -1, size)
-    zp = dot(front, left, ((0,), (0,))).astype(BF16).reshape(rows, -1, size)
-    y, z = share(yp, zp)
+    y, z = share(yp, left.T, front, rows)
     y, z = y.reshape(-1, size), z.reshape(-1, size)
     high, low = split(dot(front, z))
     both = jnp.stack([dot(y, y, ((0,), (0,))), dot(y, high, ((0,), (0,))) + dot(y, low, ((0,), (0,)))])

time: 236 us -> 203 us (0.86)
  Pallas kernels: 158 us -> 138 us
  matrix products: 72.7 us -> 58.5 us
    pallas_call x1, Pallas kernels: 95.5 us -> 80.5 us  [share(): pl.pallas_call(functools.partial(share_kernel, rows, cols, tile), out_sha...]
    dot_general x9 -> x8, matrix products: 72.7 us -> 58.5 us  [dot(): return lax.dot_general(a, b, (dims, ((), ())), preferred_element_type=F32)]
    pallas_call x1, Pallas kernels: 34.7 us -> 29.6 us  [total_of(): pl.pallas_call(functools.partial(total_kernel, rows, cols), out_shape=jax...]
where the time goes in v3:
time: 203 us; the launch traced here: 202 us
  Pallas kernels  138 us (68%)
  matrix products  58.5 us (29%)
  local copies, waits for them, and re-layouts  3.37 us (2%)
    pallas_call x1, Pallas kernels, share(): pl.pallas_call(functools.partial(share_kernel, rows, cols, tile), out_sha...  80.5 us
    dot_general x8, matrix products, dot(): return lax.dot_general(a, b, (dims, ((), ())), preferred_element_type=F32)  58.5 us
    pallas_call x1, Pallas kernels, total_of(): pl.pallas_call(functools.partial(total_kernel, rows, cols), out_shape=jax...  29.6 us
    pallas_call x1, Pallas kernels, factor(): pl.pallas_call(functools.partial(factor_kernel, order), out_shape=(shape,...  28.1 us

profile of v3, /device:TPU:0, one launch (start us, length us, event | category | flops | bytes accessed | tf_op | source)
XLA Modules:
  0.0 201.6 jit_solution(2540467295857590456)
XLA Ops:
  0.6 0.0 copy-start
  0.7 2.6 %copy.5 = bf16[2560,256]{0,1:T(8,128)(2,1)} copy(bf16[2560,256]{1,0:T(8,128)(2,1)} %param.5) | data formatting | bytes 2621440 | tf_op args[2]
  3.2 0.0 copy-done
  3.2 13.5 %fusion.9 = f32[2560,256]{1,0:T(8,128)} fusion(bf16[2560,5120]{1,0:T(8,128)(2,1)} %front_ref.1, bf16[5120,256]{1,0:T(8,128)(2,1)S(1)} %copy-done), kind=kOutput, calls=%fused_computation.18 | convolution fusion | flops 6710886400 | bytes 31457280 | tf_op jit(solution)/shard_map/dot_general | solution.py:104
  16.8 80.5 %shard_map.50 = (bf16[4,640,256]{2,1,0:T(8,128)(2,1)}, bf16[8,640,256]{2,1,0:T(8,128)(2,1)}) custom-call(f32[4,640,256]{2,1,0:T(8,128)} %bitcast.33, bf16[256,2560]{1,0:T(8,128)(2,1)} %bitcast.30, bf16[2560,5120]{1,0:T(8,128)(2,1)} %front_ref.1), custom_call_target="tpu_custom_call" | custom-call | tf_op jit(solution)/shard_map/pallas_call | solution.py:311
  97.3 0.0 copy-start.5
  97.3 2.4 %convolution_bitcast_fusion.2 = f32[1,256,256]{2,1,0:T(8,128)S(1)} fusion(bf16[4,640,256]{2,1,0:T(8,128)(2,1)} %get-tuple-element.6), kind=kOutput, calls=%fused_computation.9 | convolution fusion | flops 335544320 | bytes 1572864 | tf_op jit(solution)/shard_map/dot_general | solution.py:104
  99.7 0.1 copy-done.5
  99.8 0.9 convolution_bitcast_fusion.1
  100.7 0.6 constant_dynamic-slice_fusion.gram_ref
  101.3 0.0 copy-start.2
  101.3 14.0 %convolution_bitcast_fusion = f32[2560,256]{0,1:T(8,128)} fusion(bf16[5120,256]{1,0:T(8,128)(2,1)} %bitcast.31, bf16[2560,5120]{1,0:T(8,128)(2,1)} %front_ref.1), kind=kOutput, calls=%fused_computation.2 | convolution fusion | flops 6710886400 | bytes 31457280 | tf_op jit(solution)/shard_map/dot_general | solution.py:104
  115.3 0.0 copy-done.2
  115.3 0.0 copy-start.3
  115.3 3.3 %fusion.1 = f32[256,256]{1,0:T(8,128)S(1)} fusion(bf16[2560,256]{1,0:T(8,128)(2,1)S(1)} %bitcast.27, f32[2560,256]{0,1:T(8,128)} %convolution_bitcast_fusion), kind=kOutput, calls=%fused_computation.5 | convolution fusion | flops 338165760 | bytes 4194304 | tf_op jit(solution)/shard_map/dot_general | solution.py:104
  118.5 0.0 copy-done.3
  118.6 0.6 fusion.2
  119.2 0.8 pad_maximum_fusion.both_ref
  120.0 29.6 %shard_map.51.total_ref = f32[8,3,32,256]{3,2,1,0:T(8,128)} custom-call(f32[2,256,256]{2,1,0:T(8,128)} %pad_maximum_fusion.both_ref, f32[32,256]{1,0:T(8,128)} %constant_dynamic-slice_fusion.gram_ref), custom_call_target="tpu_custom_call" | custom-call | tf_op jit(solution)/shard_map/pallas_call | solution.py:368
  149.6 28.1 %shard_map.52 = (f32[256,256]{1,0:T(8,128)}, f32[256,256]{1,0:T(8,128)}) custom-call(f32[8,3,32,256]{3,2,1,0:T(8,128)} %shard_map.51.total_ref), custom_call_target="tpu_custom_call" | custom-call | tf_op jit(solution)/shard_map/pallas_call | solution.py:90
  177.7 0.0 copy-start.4
  177.7 3.0 %fusion.7 = f32[2560,256]{1,0:T(8,128)} fusion(bf16[2560,256]{1,0:T(8,128)(2,1)S(1)} %bitcast.29, f32[256,256]{1,0:T(8,128)} %get-tuple-element.8), kind=kOutput, calls=%fused_computation.15 | convolution fusion | flops 335609856 | bytes 4194304 | tf_op jit(solution)/shard_map/dot_general | solution.py:104
  180.7 0.0 copy-done.4
  180.7 0.0 copy-start.1
  180.7 20.9 %subtract_convert_fusion = bf16[2560,5120]{1,0:T(8,128)(2,1)} fusion(bf16[2560,5120]{1,0:T(8,128)(2,1)} %front_ref.1, bf16[5120,256]{1,0:T(8,128)(2,1)} %bitcast.32, f32[2560,256]{1,0:T(8,128)} %fusion.7, bf16[2560,256]{1,0:T(8,128)(2,1)} %bitcast.26, f32[256,256]{1,0:T(8,128)S(1)} %copy-done.4), kind=kOutput, calls=%fused_computation | convolution fusion | flops 7087325184 | bytes 59244544 | tf_op jit(solution)/shard_map/dot_general | solution.py:104
  201.6 0.0 copy-done.1
Async XLA Ops:
  0.6 2.6 %copy-start = (bf16[5120,256]{1,0:T(8,128)(2,1)S(1)}, bf16[5120,256]{1,0:T(8,128)(2,1)}, u32[]{:S(2)}) copy-start(bf16[5120,256]{1,0:T(8,128)(2,1)} %param.4) | copy-start | bytes 7864324
  97.3 2.5 %copy-start.5 = (bf16[8,640,256]{2,1,0:T(8,128)(2,1)S(1)}, bf16[8,640,256]{2,1,0:T(8,128)(2,1)}, u32[]{:S(2)}) copy-start(bf16[8,640,256]{2,1,0:T(8,128)(2,1)} %get-tuple-element.7) | copy-start | bytes 7864324
  101.3 14.0 %copy-start.2 = (bf16[4,640,256]{2,1,0:T(8,128)(2,1)S(1)}, bf16[4,640,256]{2,1,0:T(8,128)(2,1)}, u32[]{:S(2)}) copy-start(bf16[4,640,256]{2,1,0:T(8,128)(2,1)} %get-tuple-element.6) | copy-start | bytes 3932164
  115.3 3.3 %copy-start.3 = (f32[2560,256]{0,1:T(8,128)S(1)}, f32[2560,256]{0,1:T(8,128)}, u32[]{:S(2)}) copy-start(f32[2560,256]{0,1:T(8,128)} %convolution_bitcast_fusion) | copy-start | bytes 7864324
  177.7 3.0 %copy-start.4 = (f32[256,256]{1,0:T(8,128)S(1)}, f32[256,256]{1,0:T(8,128)}, u32[]{:S(2)}) copy-start(f32[256,256]{1,0:T(8,128)} %get-tuple-element.8) | copy-start | bytes 786436
  180.7 20.9 %copy-start.1 = (bf16[5120,256]{1,0:T(8,128)(2,1)S(1)}, bf16[5120,256]{1,0:T(8,128)(2,1)}, u32[]{:S(2)}) copy-start(bf16[5120,256]{1,0:T(8,128)(2,1)} %param.4) | copy-start | bytes 7864324
